TPU v7x, 32 devices: a whole 2x2x4 slice. The times are simulated.
32 devices in a mesh: groups: 2 (over x), tensor: 4 (over y, core), section: 4 (over z).
Axes of the slice: x: 2, y: 2, z: 4, core: 2. Of those that a mesh axis runs over, the one named last changes fastest.
Arguments:
- prompt: bfloat16 [128, 8192], P(('groups', 'section'), 'tensor'), parts along dimension 0, may hold values from -6 to 6
- norm_gain: float32 [8, 8192], P(('groups', 'section')), parts along dimension 0, may hold values from 0.5 to 1.5
- kept_ranks: int32 [8, 3], P(('groups', 'section')), parts along dimension 0, may hold values from 128 to 512, as said below
- gate_left: bfloat16 [8, 512, 8192], P('groups', 'tensor', 'section'), parts along dimension 0, may hold values from -0.0625 to 0.0625
- up_left: bfloat16 [8, 512, 8192], P('groups', 'tensor', 'section'), parts along dimension 0, may hold values from -0.0625 to 0.0625
- gate_right: bfloat16 [8, 512, 14336], P('groups', 'tensor', 'section'), parts along dimension 0, may hold values from -0.375 to 0.375
- up_right: bfloat16 [8, 512, 14336], P('groups', 'tensor', 'section'), parts along dimension 0, may hold values from -0.375 to 0.375
- down_left: bfloat16 [8, 512, 14336], P('groups', 'tensor', 'section'), parts along dimension 0, may hold values from -0.046875 to 0.046875
- down_right: bfloat16 [8, 8192, 512], P('groups', 'tensor', 'section'), parts along dimension 0, may hold values from -0.5 to 0.5
Outputs:
- final_stream: bfloat16 [128, 8192], P(('groups', 'section'), 'tensor'), parts along dimension 0
There are 2 independent parts, one for each index of `groups`. A program takes and returns all parts, laid end to end along the dimension named above; each array names one. Nothing has to cross between parts.
Inputs may be any that keep to these rules, and one draw needn't show every extreme that they name: `kept_ranks`: column 0, 1, 2 holds the rank kept for the gate, up and down matrices; the value 512 occurs in every draw.
All inputs are finite; a program needn't handle non-finite values.
Results may differ from a plain program's by a relative error of at most 0.035.
Values may be sent and summed in bfloat16 or wider, within the bound.
No kernel may reach another device: no remote copies, remote signals or barrier semaphores. Data moves between devices by JAX's collectives and lax.ppermute only.
A program may use at most 128 MiB of HBM per device.

v0:
```python
import jax
import jax.numpy as jnp
from jax import lax
from jax.sharding import PartitionSpec as P

RMAX = 512


def from_behind(block, axis, distance):
    devices = range(lax.axis_size(axis))
    route = [(i - distance, i) for i in devices if i - distance in devices]
    return lax.ppermute(block, axis, route)


def broadcast(array, axis, root):
    mine = lax.axis_index(axis) == root
    return lax.psum(jnp.where(mine, array, jnp.zeros_like(array)), axis)


def contract_last(left_side, right_side):
    return lax.dot_general(
        left_side, right_side, (((1,), (1,)), ((), ())), preferred_element_type=jnp.float32
    )


def body(
    prompt, norm_gain, kept_ranks, gate_left, up_left, gate_right, up_right, down_left, down_right
):
    section_count = lax.axis_size("section")
    tensor_rank = lax.axis_index("tensor")
    section_rank = lax.axis_index("section")
    gate_rows, up_rows, down_cols = (
        lax.all_to_all(gate_left, "section", split_axis=0, concat_axis=2, tiled=True),
        lax.all_to_all(up_left, "section", split_axis=0, concat_axis=2, tiled=True),
        lax.all_to_all(down_right, "section", split_axis=0, concat_axis=2, tiled=True),
    )
    gate_cols, up_cols, down_rows = (
        lax.all_to_all(
            lax.all_to_all(gate_right, "tensor", split_axis=2, concat_axis=1, tiled=True),
            "section",
            split_axis=0,
            concat_axis=2,
            tiled=True,
        ),
        lax.all_to_all(
            lax.all_to_all(up_right, "tensor", split_axis=2, concat_axis=1, tiled=True),
            "section",
            split_axis=0,
            concat_axis=2,
            tiled=True,
        ),
        lax.all_to_all(
            lax.all_to_all(down_left, "tensor", split_axis=2, concat_axis=1, tiled=True),
            "section",
            split_axis=0,
            concat_axis=2,
            tiled=True,
        ),
    )
    gate_rows, up_rows, down_cols = (gate_rows[0], up_rows[0], down_cols[0])
    gate_cols, up_cols, down_rows = (gate_cols[0], up_cols[0], down_rows[0])
    rank_block = gate_rows.shape[0]
    column_block = down_cols.shape[0]
    micro_rows = prompt.shape[0]
    positions = tensor_rank * rank_block + jnp.arange(rank_block, dtype=jnp.int32)
    gate_mask = (positions < kept_ranks[0, 0]).astype(jnp.float32)
    up_mask = (positions < kept_ranks[0, 1]).astype(jnp.float32)
    down_mask = (jnp.arange(RMAX, dtype=jnp.int32) < kept_ranks[0, 2]).astype(jnp.float32)
    norm_scale = norm_gain[0]
    own_start = tensor_rank * column_block
    prompt_rows = lax.all_gather(prompt, "section", axis=0, tiled=True)

    def layer_step(stream):
        float_stream = stream.astype(jnp.float32)
        variance = jnp.mean(float_stream * float_stream, axis=-1, keepdims=True)
        normed = (float_stream * lax.rsqrt(variance + 1e-05) * norm_scale).astype(jnp.bfloat16)
        gate_part = (contract_last(normed, gate_rows) * gate_mask).astype(jnp.bfloat16)
        up_part = (contract_last(normed, up_rows) * up_mask).astype(jnp.bfloat16)
        gate_low, up_low = (
            lax.all_gather(gate_part, "tensor", axis=1, tiled=True),
            lax.all_gather(up_part, "tensor", axis=1, tiled=True),
        )
        gate_values = jnp.dot(gate_low, gate_cols, preferred_element_type=jnp.float32)
        up_values = jnp.dot(up_low, up_cols, preferred_element_type=jnp.float32)
        hidden = (jax.nn.silu(gate_values) * up_values).astype(jnp.bfloat16)
        summed = lax.psum(contract_last(hidden, down_rows), "tensor")
        down_low = (summed * down_mask).astype(jnp.bfloat16)
        branch = contract_last(down_low, down_cols)
        own_columns = lax.dynamic_slice_in_dim(float_stream, own_start, column_block, 1)
        return (own_columns + branch).astype(jnp.bfloat16)

    incoming = jnp.zeros((micro_rows, column_block), jnp.bfloat16)
    results = jnp.zeros((micro_rows * section_count, column_block), jnp.bfloat16)

    def tick_body(tick_index, carry):
        incoming, results = carry
        entering = lax.dynamic_slice_in_dim(
            prompt_rows, jnp.minimum(tick_index, section_count - 1) * micro_rows, micro_rows, 0
        )
        current = jnp.where((section_rank == 0) & (tick_index < section_count), entering, incoming)
        stream = lax.all_gather(current, "tensor", axis=1, tiled=True)
        new_part = layer_step(stream)
        incoming = from_behind(new_part, "section", 1)
        finished = tick_index - (section_count - 1)
        slot_start = jnp.maximum(finished, 0) * micro_rows
        updated = lax.dynamic_update_slice_in_dim(results, new_part, slot_start, 0)
        results = jnp.where((section_rank == section_count - 1) & (finished >= 0), updated, results)
        return (incoming, results)

    incoming, results = lax.fori_loop(0, 2 * section_count - 1, tick_body, (incoming, results))
    delivered = broadcast(results, "section", section_count - 1)
    return lax.dynamic_slice_in_dim(delivered, section_rank * micro_rows, micro_rows, 0)


def solution(mesh):
    in_specs = (
        P(("groups", "section"), "tensor"),
        P(("groups", "section"), None),
        P(("groups", "section"), None),
        P("groups", "tensor", "section"),
        P("groups", "tensor", "section"),
        P("groups", "tensor", "section"),
        P("groups", "tensor", "section"),
        P("groups", "tensor", "section"),
        P("groups", "tensor", "section"),
    )
    out_specs = P(("groups", "section"), "tensor")
    return jax.shard_map(body, mesh=mesh, in_specs=in_specs, out_specs=out_specs, check_vma=False)
```

profile of v0, /device:TPU:0, one launch (start us, length us, event | category | flops | bytes accessed | tf_op | source)
XLA Modules:
  0.0 1003.2 jit_solution(816205238414276463)
XLA Ops:
  6.5 6.8 copy.26
  13.4 4.8 all-to-all-start.1
  18.2 6.9 copy.30
  25.0 36.4 %all-to-all-done.1 = bf16[4,128,3584]{1,0,2:T(4,128)(2,1)} async-done(((bf16[4,128,3584]{1,0,2:T(4,128)(2,1)}), bf16[4,128,3584]{1,0,2:T(4,128)(2,1)}, u32[]{:S(2)}, u32[]{:S(2)}) %all-to-all-start.1) | async-done | bytes 3670048 | tf_op jit(solution)/shard_map/all_to_all | solution.py:39
  61.4 4.7 all-to-all-start.4
  66.2 6.9 copy.33
  73.0 35.7 %all-to-all-done.4 = bf16[4,128,3584]{1,0,2:T(4,128)(2,1)} async-done(((bf16[4,128,3584]{1,0,2:T(4,128)(2,1)}), bf16[4,128,3584]{1,0,2:T(4,128)(2,1)}, u32[]{:S(2)}, u32[]{:S(2)}) %all-to-all-start.4) | async-done | bytes 3670048 | tf_op jit(solution)/shard_map/all_to_all | solution.py:46
  108.7 48.1 %all_to_all.144 = bf16[4,128,3584]{1,0,2:T(4,128)(2,1)} all-to-all(bf16[4,128,3584]{1,0,2:T(4,128)(2,1)} %copy.33), channel_id=1, replica_groups=mesh['groups'=2,'tensor'=4,'section'=4] {'tensor'}, dimensions={2} | all-to-all | bytes 7340032 | tf_op jit(solution)/shard_map/all_to_all | solution.py:53
  156.8 53.6 %all_to_all.145 = bf16[4,128,2048]{2,1,0:T(8,128)(2,1)} all-to-all(bf16[4,128,2048]{2,1,0:T(8,128)(2,1)S(1)} %copy-done.6), channel_id=1, replica_groups=mesh['groups'=2,'tensor'=4,'section'=4] {'section'}, dimensions={0} | all-to-all | bytes 4194304 | tf_op jit(solution)/shard_map/all_to_all | solution.py:33
  210.4 50.4 %all_to_all.146 = bf16[4,128,2048]{2,1,0:T(8,128)(2,1)} all-to-all(bf16[4,128,2048]{2,1,0:T(8,128)(2,1)S(1)} %copy-done.7), channel_id=1, replica_groups=mesh['groups'=2,'tensor'=4,'section'=4] {'section'}, dimensions={0} | all-to-all | bytes 4194304 | tf_op jit(solution)/shard_map/all_to_all | solution.py:34
  264.5 6.9 copy.27
  271.3 40.4 %all-to-all-done.8 = bf16[4,2048,128]{2,1,0:T(8,128)(2,1)S(1)} async-done(((bf16[4,2048,128]{2,1,0:T(8,128)(2,1)}), bf16[4,2048,128]{2,1,0:T(8,128)(2,1)S(1)}, u32[]{:S(2)}, u32[]{:S(2)}) %all-to-all-start.8) | async-done | bytes 2097184 | tf_op jit(solution)/shard_map/all_to_all | solution.py:35
  313.0 4.8 all-to-all-start.2
  317.8 6.9 copy.31
  324.7 74.6 %all-to-all-done.2 = bf16[4,512,896]{2,1,0:T(8,128)(2,1)} async-done(((bf16[4,512,896]{2,1,0:T(8,128)(2,1)}), bf16[4,512,896]{2,1,0:T(8,128)(2,1)}, u32[]{:S(2)}, u32[]{:S(2)}) %all-to-all-start.2) | async-done | bytes 3670048 | tf_op jit(solution)/shard_map/all_to_all | solution.py:38
  399.3 4.7 all-to-all-start.5
  404.1 7.0 copy.34
  411.0 74.6 %all-to-all-done.5 = bf16[4,512,896]{2,1,0:T(8,128)(2,1)} async-done(((bf16[4,512,896]{2,1,0:T(8,128)(2,1)}), bf16[4,512,896]{2,1,0:T(8,128)(2,1)}, u32[]{:S(2)}, u32[]{:S(2)}) %all-to-all-start.5) | async-done | bytes 3670048 | tf_op jit(solution)/shard_map/all_to_all | solution.py:45
  485.6 4.9 all-to-all-start.7
  490.6 89.0 %all_gather.33 = bf16[64,2048]{1,0:T(8,128)(2,1)S(1)} all-gather(bf16[16,2048]{1,0:T(8,128)(2,1)S(1)} %copy-done.8), channel_id=1, replica_groups=mesh['groups'=2,'tensor'=4,'section'=4] {'section'}, dimensions={0}, use_global_device_ids=true | all-gather | bytes 327680 | tf_op jit(solution)/shard_map/all_gather | solution.py:71
  587.6 9.7 copy.36
  599.1 6.0 copy.28
  605.0 5.9 copy.37
  611.0 6.0 copy.32
  616.9 6.0 copy.38
  622.9 6.0 copy.35
  628.9 6.0 copy.39
  634.9 322.3 %while.19 = (s32[]{:T(128)}, bf16[16,2048]{1,0:T(8,128)(2,1)S(1)}, bf16[64,2048]{1,0:T(8,128)(2,1)S(1)}, pred[]{:T(512)}, bf16[64,2048]{1,0:T(8,128)(2,1)S(1)}, ...) while((s32[]{:T(128)}, bf16[16,2048]{1,0:T(8,128)(2,1)S(1)}, ...), condition=%wide.region_3.4_spmd.clone.clone, body=%wide.region_0.3_spmd.clone.clone.sunk | while | flops 278906656 | bytes 35412760 | solution.py:110
  635.0 5.8 all_gather.43
  642.5 5.2 all_gather.45
  650.6 5.2 all_gather.44
  656.4 4.7 fusion.54
  661.0 11.4 %psum.25 = f32[16,512]{1,0:T(8,128)S(1)} all-reduce(f32[16,512]{1,0:T(8,128)S(1)} %fusion.54), channel_id=1, replica_groups=mesh['groups'=2,'tensor'=4,'section'=4] {'tensor'}, use_global_device_ids=true, to_apply=%region_2.2 | all-reduce | flops 8192 | bytes 65536 | tf_op jit(solution)/shard_map/while/body/eval_jaxpr/psum | solution.py:86
  680.1 5.8 all_gather.43
  687.6 5.2 all_gather.45
  695.7 5.2 all_gather.44
  701.4 4.7 fusion.54
  706.1 10.9 %psum.25 = f32[16,512]{1,0:T(8,128)S(1)} all-reduce(f32[16,512]{1,0:T(8,128)S(1)} %fusion.54), channel_id=1, replica_groups=mesh['groups'=2,'tensor'=4,'section'=4] {'tensor'}, use_global_device_ids=true, to_apply=%region_2.2 | all-reduce | flops 8192 | bytes 65536 | tf_op jit(solution)/shard_map/while/body/eval_jaxpr/psum | solution.py:86
  726.0 5.8 all_gather.43
  733.5 5.2 all_gather.45
  741.6 5.2 all_gather.44
  747.4 4.7 fusion.54
  752.1 11.4 %psum.25 = f32[16,512]{1,0:T(8,128)S(1)} all-reduce(f32[16,512]{1,0:T(8,128)S(1)} %fusion.54), channel_id=1, replica_groups=mesh['groups'=2,'tensor'=4,'section'=4] {'tensor'}, use_global_device_ids=true, to_apply=%region_2.2 | all-reduce | flops 8192 | bytes 65536 | tf_op jit(solution)/shard_map/while/body/eval_jaxpr/psum | solution.py:86
  772.5 5.8 all_gather.43
  780.0 5.2 all_gather.45
  788.1 5.2 all_gather.44
  793.8 4.7 fusion.54
  798.5 10.9 %psum.25 = f32[16,512]{1,0:T(8,128)S(1)} all-reduce(f32[16,512]{1,0:T(8,128)S(1)} %fusion.54), channel_id=1, replica_groups=mesh['groups'=2,'tensor'=4,'section'=4] {'tensor'}, use_global_device_ids=true, to_apply=%region_2.2 | all-reduce | flops 8192 | bytes 65536 | tf_op jit(solution)/shard_map/while/body/eval_jaxpr/psum | solution.py:86
  818.4 5.8 all_gather.43
  825.9 5.2 all_gather.45
  834.0 5.2 all_gather.44
  839.8 4.7 fusion.54
  844.5 11.4 %psum.25 = f32[16,512]{1,0:T(8,128)S(1)} all-reduce(f32[16,512]{1,0:T(8,128)S(1)} %fusion.54), channel_id=1, replica_groups=mesh['groups'=2,'tensor'=4,'section'=4] {'tensor'}, use_global_device_ids=true, to_apply=%region_2.2 | all-reduce | flops 8192 | bytes 65536 | tf_op jit(solution)/shard_map/while/body/eval_jaxpr/psum | solution.py:86
  864.9 5.8 all_gather.43
  872.4 5.2 all_gather.45
  880.5 5.2 all_gather.44
  886.2 4.7 fusion.54
  890.9 10.9 %psum.25 = f32[16,512]{1,0:T(8,128)S(1)} all-reduce(f32[16,512]{1,0:T(8,128)S(1)} %fusion.54), channel_id=1, replica_groups=mesh['groups'=2,'tensor'=4,'section'=4] {'tensor'}, use_global_device_ids=true, to_apply=%region_2.2 | all-reduce | flops 8192 | bytes 65536 | tf_op jit(solution)/shard_map/while/body/eval_jaxpr/psum | solution.py:86
  910.8 5.8 all_gather.43
  918.3 5.2 all_gather.45
  926.4 5.2 all_gather.44
  932.2 4.7 fusion.54
  936.9 11.4 %psum.25 = f32[16,512]{1,0:T(8,128)S(1)} all-reduce(f32[16,512]{1,0:T(8,128)S(1)} %fusion.54), channel_id=1, replica_groups=mesh['groups'=2,'tensor'=4,'section'=4] {'tensor'}, use_global_device_ids=true, to_apply=%region_2.2 | all-reduce | flops 8192 | bytes 65536 | tf_op jit(solution)/shard_map/while/body/eval_jaxpr/psum | solution.py:86
  958.0 36.9 %all-reduce.2.cloned.1.call-done = bf16[64,2048]{1,0:T(8,128)(2,1)} async-done(((bf16[64,2048]{1,0:T(8,128)(2,1)}), bf16[64,2048]{1,0:T(8,128)(2,1)}) %all-reduce.2.cloned.1.call-update) | async-done | bytes 262160 | tf_op jit(solution)/shard_map/psum | solution.py:17
  (137 shorter events, 114.8 us)
Async XLA Ops:
  13.4 48.0 %all-to-all-start.1 = ((bf16[4,128,3584]{1,0,2:T(4,128)(2,1)}), bf16[4,128,3584]{1,0,2:T(4,128)(2,1)}, u32[]{:S(2)}, u32[]{:S(2)}) async-start(bf16[4,128,3584]{1,0,2:T(4,128)(2,1)} %copy.26), calls=%async_computation.1 | async-start | bytes 7340032 | tf_op jit(solution)/shard_map/all_to_all | solution.py:39
  61.4 47.3 %all-to-all-start.4 = ((bf16[4,128,3584]{1,0,2:T(4,128)(2,1)}), bf16[4,128,3584]{1,0,2:T(4,128)(2,1)}, u32[]{:S(2)}, u32[]{:S(2)}) async-start(bf16[4,128,3584]{1,0,2:T(4,128)(2,1)} %copy.30), calls=%async_computation.4 | async-start | bytes 7340032 | tf_op jit(solution)/shard_map/all_to_all | solution.py:46
  73.0 83.8 %copy-start.6 = (bf16[4,128,2048]{2,1,0:T(8,128)(2,1)S(1)}, bf16[4,128,2048]{2,1,0:T(8,128)(2,1)}, u32[]{:S(2)}) copy-start(bf16[4,128,2048]{2,1,0:T(8,128)(2,1)} %param.14) | copy-start | bytes 6291460
  156.8 53.6 %copy-start.7 = (bf16[4,128,2048]{2,1,0:T(8,128)(2,1)S(1)}, bf16[4,128,2048]{2,1,0:T(8,128)(2,1)}, u32[]{:S(2)}) copy-start(bf16[4,128,2048]{2,1,0:T(8,128)(2,1)} %param.15) | copy-start | bytes 6291460
  260.8 50.9 %all-to-all-start.8 = ((bf16[4,2048,128]{2,1,0:T(8,128)(2,1)}), bf16[4,2048,128]{2,1,0:T(8,128)(2,1)S(1)}, u32[]{:S(2)}, u32[]{:S(2)}) async-start(bf16[4,2048,128]{2,1,0:T(8,128)(2,1)} %param.19), calls=%async_computation.8 | async-start | bytes 4194304 | tf_op jit(solution)/shard_map/all_to_all | solution.py:35
  311.7 1.3 copy-start.1
  313.0 86.3 %all-to-all-start.2 = ((bf16[4,512,896]{2,1,0:T(8,128)(2,1)}), bf16[4,512,896]{2,1,0:T(8,128)(2,1)}, u32[]{:S(2)}, u32[]{:S(2)}) async-start(bf16[4,512,896]{2,1,0:T(8,128)(2,1)} %bitcast.83), calls=%async_computation.2 | async-start | bytes 7340032 | tf_op jit(solution)/shard_map/all_to_all | solution.py:38
  399.3 86.3 %all-to-all-start.5 = ((bf16[4,512,896]{2,1,0:T(8,128)(2,1)}), bf16[4,512,896]{2,1,0:T(8,128)(2,1)}, u32[]{:S(2)}, u32[]{:S(2)}) async-start(bf16[4,512,896]{2,1,0:T(8,128)(2,1)} %bitcast.82), calls=%async_computation.5 | async-start | bytes 7340032 | tf_op jit(solution)/shard_map/all_to_all | solution.py:45
  485.6 5.0 copy-start.8
  485.6 94.0 %copy-start.9 = (s32[1,3]{1,0:T(1,128)S(1)}, s32[1,3]{1,0:T(1,128)}, u32[]{:S(2)}) copy-start(s32[1,3]{1,0:T(1,128)} %param.13) | copy-start | bytes 40
  485.6 94.6 %copy-start.4 = (bf16[4,128,2048]{2,1,0:T(8,128)(2,1)S(1)}, bf16[4,128,2048]{2,1,0:T(8,128)(2,1)}, u32[]{:S(2)}) copy-start(bf16[4,128,2048]{2,1,0:T(8,128)(2,1)} %all_to_all.145) | copy-start | bytes 6291460
  485.6 137.3 %all-to-all-start.7 = ((bf16[4,512,896]{2,1,0:T(8,128)(2,1)}), bf16[4,512,896]{2,1,0:T(8,128)(2,1)}, u32[]{:S(2)}, u32[]{:S(2)}) async-start(bf16[4,512,896]{2,1,0:T(8,128)(2,1)} %bitcast.80), calls=%async_computation.7 | async-start | bytes 7340032 | tf_op jit(solution)/shard_map/all_to_all | solution.py:52
  490.5 504.4 %all-reduce.2.cloned.1.call-start = ((), (), s32[]{:S(2)}) async-start(), calls=%async_computation.9 | async-start | bytes 524288 | tf_op jit(solution)/shard_map/psum | solution.py:17
  580.2 3.1 copy-start.3
  583.3 4.4 copy-start.2
  628.9 6.0 copy-start.5
  641.0 14.8 %copy-start = (bf16[512,3584]{1,0:T(8,128)(2,1)S(1)}, bf16[512,3584]{1,0:T(8,128)(2,1)}, u32[]{:S(2)}) copy-start(bf16[512,3584]{1,0:T(8,128)(2,1)} %get-tuple-element.710) | copy-start | bytes 11010052 | tf_op jit(solution)/shard_map/while
  675.3 4.8 collective-permute-start
  686.1 14.8 %copy-start = (bf16[512,3584]{1,0:T(8,128)(2,1)S(1)}, bf16[512,3584]{1,0:T(8,128)(2,1)}, u32[]{:S(2)}) copy-start(bf16[512,3584]{1,0:T(8,128)(2,1)} %get-tuple-element.710) | copy-start | bytes 11010052 | tf_op jit(solution)/shard_map/while
  719.8 6.2 collective-permute-start
  732.0 14.8 %copy-start = (bf16[512,3584]{1,0:T(8,128)(2,1)S(1)}, bf16[512,3584]{1,0:T(8,128)(2,1)}, u32[]{:S(2)}) copy-start(bf16[512,3584]{1,0:T(8,128)(2,1)} %get-tuple-element.710) | copy-start | bytes 11010052 | tf_op jit(solution)/shard_map/while
  766.3 6.2 collective-permute-start
  778.5 14.8 %copy-start = (bf16[512,3584]{1,0:T(8,128)(2,1)S(1)}, bf16[512,3584]{1,0:T(8,128)(2,1)}, u32[]{:S(2)}) copy-start(bf16[512,3584]{1,0:T(8,128)(2,1)} %get-tuple-element.710) | copy-start | bytes 11010052 | tf_op jit(solution)/shard_map/while
  812.2 6.2 collective-permute-start
  824.4 14.8 %copy-start = (bf16[512,3584]{1,0:T(8,128)(2,1)S(1)}, bf16[512,3584]{1,0:T(8,128)(2,1)}, u32[]{:S(2)}) copy-start(bf16[512,3584]{1,0:T(8,128)(2,1)} %get-tuple-element.710) | copy-start | bytes 11010052 | tf_op jit(solution)/shard_map/while
  858.7 6.2 collective-permute-start
  870.9 14.8 %copy-start = (bf16[512,3584]{1,0:T(8,128)(2,1)S(1)}, bf16[512,3584]{1,0:T(8,128)(2,1)}, u32[]{:S(2)}) copy-start(bf16[512,3584]{1,0:T(8,128)(2,1)} %get-tuple-element.710) | copy-start | bytes 11010052 | tf_op jit(solution)/shard_map/while
  904.6 6.2 collective-permute-start
  916.8 14.8 %copy-start = (bf16[512,3584]{1,0:T(8,128)(2,1)S(1)}, bf16[512,3584]{1,0:T(8,128)(2,1)}, u32[]{:S(2)}) copy-start(bf16[512,3584]{1,0:T(8,128)(2,1)} %get-tuple-element.710) | copy-start | bytes 11010052 | tf_op jit(solution)/shard_map/while
  951.1 6.2 collective-permute-start
Sparse Core Ops, SparseCore 0:
  958.1 36.7 all-reduce.1
where the time goes:
time: 1010 us; the launch traced here: 1000 us
  blocking collectives  432 us (43%)
  waiting for transfers between devices  312 us (31%)
  local copies, waits for them, and re-layouts  99.4 us (10%)
  matrix products  73.3 us (7%)
  starting transfers between devices  56.1 us (6%)
  other arithmetic  16.3 us (2%)
  between operations  13.5 us (1%)
    all_gather x1, blocking collectives, body(): prompt_rows = lax.all_gather(prompt, 'section', axis=0, tiled=True)  89 us
    psum x7, blocking collectives, layer_step(): summed = lax.psum(contract_last(hidden, down_rows), 'tensor')  78.1 us
    all_to_all x1, waiting for transfers between devices, body(): lax.all_to_all(lax.all_to_all(gate_right, 'tensor', split_axis=2, concat_...  74.6 us
    all_to_all x1, waiting for transfers between devices, body(): lax.all_to_all(lax.all_to_all(up_right, 'tensor', split_axis=2, concat_ax...  74.6 us
    dot_general x28, matrix products, contract_last(): lax.dot_general(left_side, right_side, (((1,), (1,)), ((), ())), preferre...  69.2 us
    all_to_all x1, blocking collectives, body(): lax.all_to_all(gate_left, 'section', split_axis=0, concat_axis=2, tiled=T...  53.6 us
    all_to_all x1, blocking collectives, body(): lax.all_to_all(up_left, 'section', split_axis=0, concat_axis=2, tiled=True)  50.4 us
    all_to_all x1, blocking collectives, body(): lax.all_to_all(down_left, 'tensor', split_axis=2, concat_axis=1, tiled=True)  48.1 us
  transfers between devices with their start and end apart: 14, of which 13 were waited for; matrix products, arithmetic and copies ran while one was open for 8% of the time, Pallas kernels for 0%

commit v1 on v0

--- a/solution.py
+++ b/solution.py
@@ -2,6 +2,7 @@
 import jax.numpy as jnp
 from jax import lax
 from jax.sharding import PartitionSpec as P
+from jax.lax import all_gather
 
 RMAX = 512
 
@@ -83,7 +84,8 @@
         gate_values = jnp.dot(gate_low, gate_cols, preferred_element_type=jnp.float32)
         up_values = jnp.dot(up_low, up_cols, preferred_element_type=jnp.float32)
         hidden = (jax.nn.silu(gate_values) * up_values).astype(jnp.bfloat16)
-        summed = lax.psum(contract_last(hidden, down_rows), "tensor")
+        values = contract_last(hidden, down_rows)
+        summed = all_gather(values, axis_name="tensor").sum(axis=0)
         down_low = (summed * down_mask).astype(jnp.bfloat16)
         branch = contract_last(down_low, down_cols)
         own_columns = lax.dynamic_slice_in_dim(float_stream, own_start, column_block, 1)

time: 1010 us -> 967 us (0.957)
  blocking collectives: 432 us -> 392 us
    psum x7 -> x0, blocking collectives: 78.1 us -> none  [layer_step(): summed = lax.psum(contract_last(hidden, down_rows), 'tensor')]
    all_gather x0 -> x7, blocking collectives: none -> 38 us  [layer_step(): summed = all_gather(values, axis_name='tensor').sum(axis=0)]
where the time goes in v1:
time: 967 us; the launch traced here: 964 us
  blocking collectives  392 us (41%)
  waiting for transfers between devices  312 us (32%)
  local copies, waits for them, and re-layouts  99.4 us (10%)
  matrix products  73.3 us (8%)
  starting transfers between devices  56.6 us (6%)
  other arithmetic  16.4 us (2%)
  between operations  13.5 us (1%)
    all_gather x1, blocking collectives, body(): prompt_rows = lax.all_gather(prompt, 'section', axis=0, tiled=True)  89 us
    all_to_all x1, waiting for transfers between devices, body(): lax.all_to_all(lax.all_to_all(gate_right, 'tensor', split_axis=2, concat_...  74.6 us
    all_to_all x1, waiting for transfers between devices, body(): lax.all_to_all(lax.all_to_all(up_right, 'tensor', split_axis=2, concat_ax...  74.6 us
    dot_general x28, matrix products, contract_last(): lax.dot_general(left_side, right_side, (((1,), (1,)), ((), ())), preferre...  69.2 us
    all_to_all x1, blocking collectives, body(): lax.all_to_all(gate_left, 'section', split_axis=0, concat_axis=2, tiled=T...  53.6 us
    all_to_all x1, blocking collectives, body(): lax.all_to_all(up_left, 'section', split_axis=0, concat_axis=2, tiled=True)  50.4 us
    all_to_all x1, blocking collectives, body(): lax.all_to_all(down_left, 'tensor', split_axis=2, concat_axis=1, tiled=True)  48.1 us
    unnamed x27, local copies, waits for them, and re-layouts  45.7 us
  transfers between devices with their start and end apart: 14, of which 13 were waited for; matrix products, arithmetic and copies ran while one was open for 8% of the time, Pallas kernels for 0%

profile of v1, /device:TPU:0, one launch (start us, length us, event | category | flops | bytes accessed | tf_op | source)
XLA Modules:
  0.0 964.2 jit_solution(6980734389071341305)
XLA Ops:
  6.5 6.8 copy.26
  13.4 4.8 all-to-all-start.1
  18.2 6.9 copy.30
  25.0 36.4 %all-to-all-done.1 = bf16[4,128,3584]{1,0,2:T(4,128)(2,1)} async-done(((bf16[4,128,3584]{1,0,2:T(4,128)(2,1)}), bf16[4,128,3584]{1,0,2:T(4,128)(2,1)}, u32[]{:S(2)}, u32[]{:S(2)}) %all-to-all-start.1) | async-done | bytes 3670048 | tf_op jit(solution)/shard_map/all_to_all | solution.py:40
  61.4 4.7 all-to-all-start.4
  66.2 6.9 copy.33
  73.0 35.7 %all-to-all-done.4 = bf16[4,128,3584]{1,0,2:T(4,128)(2,1)} async-done(((bf16[4,128,3584]{1,0,2:T(4,128)(2,1)}), bf16[4,128,3584]{1,0,2:T(4,128)(2,1)}, u32[]{:S(2)}, u32[]{:S(2)}) %all-to-all-start.4) | async-done | bytes 3670048 | tf_op jit(solution)/shard_map/all_to_all | solution.py:47
  108.7 48.1 %all_to_all.144 = bf16[4,128,3584]{1,0,2:T(4,128)(2,1)} all-to-all(bf16[4,128,3584]{1,0,2:T(4,128)(2,1)} %copy.33), channel_id=1, replica_groups=mesh['groups'=2,'tensor'=4,'section'=4] {'tensor'}, dimensions={2} | all-to-all | bytes 7340032 | tf_op jit(solution)/shard_map/all_to_all | solution.py:54
  156.8 53.6 %all_to_all.145 = bf16[4,128,2048]{2,1,0:T(8,128)(2,1)} all-to-all(bf16[4,128,2048]{2,1,0:T(8,128)(2,1)S(1)} %copy-done.6), channel_id=1, replica_groups=mesh['groups'=2,'tensor'=4,'section'=4] {'section'}, dimensions={0} | all-to-all | bytes 4194304 | tf_op jit(solution)/shard_map/all_to_all | solution.py:34
  210.4 50.4 %all_to_all.146 = bf16[4,128,2048]{2,1,0:T(8,128)(2,1)} all-to-all(bf16[4,128,2048]{2,1,0:T(8,128)(2,1)S(1)} %copy-done.7), channel_id=1, replica_groups=mesh['groups'=2,'tensor'=4,'section'=4] {'section'}, dimensions={0} | all-to-all | bytes 4194304 | tf_op jit(solution)/shard_map/all_to_all | solution.py:35
  264.5 6.9 copy.27
  271.3 40.4 %all-to-all-done.8 = bf16[4,2048,128]{2,1,0:T(8,128)(2,1)S(1)} async-done(((bf16[4,2048,128]{2,1,0:T(8,128)(2,1)}), bf16[4,2048,128]{2,1,0:T(8,128)(2,1)S(1)}, u32[]{:S(2)}, u32[]{:S(2)}) %all-to-all-start.8) | async-done | bytes 2097184 | tf_op jit(solution)/shard_map/all_to_all | solution.py:36
  313.0 4.8 all-to-all-start.2
  317.8 6.9 copy.31
  324.7 74.6 %all-to-all-done.2 = bf16[4,512,896]{2,1,0:T(8,128)(2,1)} async-done(((bf16[4,512,896]{2,1,0:T(8,128)(2,1)}), bf16[4,512,896]{2,1,0:T(8,128)(2,1)}, u32[]{:S(2)}, u32[]{:S(2)}) %all-to-all-start.2) | async-done | bytes 3670048 | tf_op jit(solution)/shard_map/all_to_all | solution.py:39
  399.3 4.7 all-to-all-start.5
  404.1 7.0 copy.34
  411.0 74.6 %all-to-all-done.5 = bf16[4,512,896]{2,1,0:T(8,128)(2,1)} async-done(((bf16[4,512,896]{2,1,0:T(8,128)(2,1)}), bf16[4,512,896]{2,1,0:T(8,128)(2,1)}, u32[]{:S(2)}, u32[]{:S(2)}) %all-to-all-start.5) | async-done | bytes 3670048 | tf_op jit(solution)/shard_map/all_to_all | solution.py:46
  485.6 4.9 all-to-all-start.7
  490.6 89.0 %all_gather.53 = bf16[64,2048]{1,0:T(8,128)(2,1)S(1)} all-gather(bf16[16,2048]{1,0:T(8,128)(2,1)S(1)} %copy-done.8), channel_id=1, replica_groups=mesh['groups'=2,'tensor'=4,'section'=4] {'section'}, dimensions={0}, use_global_device_ids=true | all-gather | bytes 327680 | tf_op jit(solution)/shard_map/all_gather | solution.py:72
  587.6 9.7 %copy.36 = bf16[1,2048,4,128]{3,2,1,0:T(4,128)(2,1)S(1)} copy(bf16[1,2048,4,128]{3,1,2,0:T(8,128)(2,1)S(1)} %bitcast.91) | data formatting | bytes 4194304 | tf_op jit(solution)/shard_map/all_to_all | solution.py:36
  599.1 6.0 copy.28
  605.0 5.9 copy.37
  611.0 6.0 copy.32
  616.9 6.0 copy.38
  622.9 6.0 copy.35
  628.9 6.0 copy.39
  634.9 282.7 %while.19 = (s32[]{:T(128)}, bf16[16,2048]{1,0:T(8,128)(2,1)S(1)}, bf16[64,2048]{1,0:T(8,128)(2,1)S(1)}, pred[]{:T(512)}, bf16[64,2048]{1,0:T(8,128)(2,1)S(1)}, ...) while((s32[]{:T(128)}, bf16[16,2048]{1,0:T(8,128)(2,1)S(1)}, ...), condition=%wide.region_3.4_spmd.clone.clone, body=%wide.region_0.3_spmd.clone.clone.sunk | while | flops 278923040 | bytes 35674916 | solution.py:112
  635.0 5.8 all_gather.63
  642.5 5.2 all_gather.65
  650.6 5.2 all_gather.64
  656.4 4.7 fusion.54
  661.0 5.4 all-gather.4
  674.1 5.8 all_gather.63
  681.6 5.2 all_gather.65
  689.7 5.2 all_gather.64
  695.5 4.7 fusion.54
  700.2 5.4 all-gather.4
  714.7 5.8 all_gather.63
  722.2 5.2 all_gather.65
  730.3 5.2 all_gather.64
  736.1 4.7 fusion.54
  740.8 5.4 all-gather.4
  755.3 5.8 all_gather.63
  762.8 5.2 all_gather.65
  770.9 5.2 all_gather.64
  776.7 4.7 fusion.54
  781.4 5.4 all-gather.4
  795.9 5.8 all_gather.63
  803.4 5.2 all_gather.65
  811.5 5.2 all_gather.64
  817.3 4.7 fusion.54
  822.0 5.4 all-gather.4
  836.5 5.8 all_gather.63
  844.0 5.2 all_gather.65
  852.1 5.2 all_gather.64
  857.9 4.7 fusion.54
  862.5 5.4 all-gather.4
  877.1 5.8 all_gather.63
  884.6 5.2 all_gather.65
  892.7 5.2 all_gather.64
  898.4 4.7 fusion.54
  903.1 5.4 all-gather.4
  918.4 37.5 %all-reduce.2.cloned.1.call-done = bf16[64,2048]{1,0:T(8,128)(2,1)} async-done(((bf16[64,2048]{1,0:T(8,128)(2,1)}), bf16[64,2048]{1,0:T(8,128)(2,1)}) %all-reduce.2.cloned.1.call-update) | async-done | bytes 262160 | tf_op jit(solution)/shard_map/psum | solution.py:18
  (144 shorter events, 115.3 us)
Async XLA Ops:
  13.4 48.0 %all-to-all-start.1 = ((bf16[4,128,3584]{1,0,2:T(4,128)(2,1)}), bf16[4,128,3584]{1,0,2:T(4,128)(2,1)}, u32[]{:S(2)}, u32[]{:S(2)}) async-start(bf16[4,128,3584]{1,0,2:T(4,128)(2,1)} %copy.26), calls=%async_computation.1 | async-start | bytes 7340032 | tf_op jit(solution)/shard_map/all_to_all | solution.py:40
  61.4 47.3 %all-to-all-start.4 = ((bf16[4,128,3584]{1,0,2:T(4,128)(2,1)}), bf16[4,128,3584]{1,0,2:T(4,128)(2,1)}, u32[]{:S(2)}, u32[]{:S(2)}) async-start(bf16[4,128,3584]{1,0,2:T(4,128)(2,1)} %copy.30), calls=%async_computation.4 | async-start | bytes 7340032 | tf_op jit(solution)/shard_map/all_to_all | solution.py:47
  73.0 83.8 %copy-start.6 = (bf16[4,128,2048]{2,1,0:T(8,128)(2,1)S(1)}, bf16[4,128,2048]{2,1,0:T(8,128)(2,1)}, u32[]{:S(2)}) copy-start(bf16[4,128,2048]{2,1,0:T(8,128)(2,1)} %param.14) | copy-start | bytes 6291460
  156.8 53.6 %copy-start.7 = (bf16[4,128,2048]{2,1,0:T(8,128)(2,1)S(1)}, bf16[4,128,2048]{2,1,0:T(8,128)(2,1)}, u32[]{:S(2)}) copy-start(bf16[4,128,2048]{2,1,0:T(8,128)(2,1)} %param.15) | copy-start | bytes 6291460
  260.8 50.9 %all-to-all-start.8 = ((bf16[4,2048,128]{2,1,0:T(8,128)(2,1)}), bf16[4,2048,128]{2,1,0:T(8,128)(2,1)S(1)}, u32[]{:S(2)}, u32[]{:S(2)}) async-start(bf16[4,2048,128]{2,1,0:T(8,128)(2,1)} %param.19), calls=%async_computation.8 | async-start | bytes 4194304 | tf_op jit(solution)/shard_map/all_to_all | solution.py:36
  311.7 1.3 copy-start.1
  313.0 86.3 %all-to-all-start.2 = ((bf16[4,512,896]{2,1,0:T(8,128)(2,1)}), bf16[4,512,896]{2,1,0:T(8,128)(2,1)}, u32[]{:S(2)}, u32[]{:S(2)}) async-start(bf16[4,512,896]{2,1,0:T(8,128)(2,1)} %bitcast.86), calls=%async_computation.2 | async-start | bytes 7340032 | tf_op jit(solution)/shard_map/all_to_all | solution.py:39
  399.3 86.3 %all-to-all-start.5 = ((bf16[4,512,896]{2,1,0:T(8,128)(2,1)}), bf16[4,512,896]{2,1,0:T(8,128)(2,1)}, u32[]{:S(2)}, u32[]{:S(2)}) async-start(bf16[4,512,896]{2,1,0:T(8,128)(2,1)} %bitcast.85), calls=%async_computation.5 | async-start | bytes 7340032 | tf_op jit(solution)/shard_map/all_to_all | solution.py:46
  485.6 5.0 copy-start.8
  485.6 94.0 %copy-start.9 = (s32[1,3]{1,0:T(1,128)S(1)}, s32[1,3]{1,0:T(1,128)}, u32[]{:S(2)}) copy-start(s32[1,3]{1,0:T(1,128)} %param.13) | copy-start | bytes 40
  485.6 94.6 %copy-start.4 = (bf16[4,128,2048]{2,1,0:T(8,128)(2,1)S(1)}, bf16[4,128,2048]{2,1,0:T(8,128)(2,1)}, u32[]{:S(2)}) copy-start(bf16[4,128,2048]{2,1,0:T(8,128)(2,1)} %all_to_all.145) | copy-start | bytes 6291460
  485.6 137.3 %all-to-all-start.7 = ((bf16[4,512,896]{2,1,0:T(8,128)(2,1)}), bf16[4,512,896]{2,1,0:T(8,128)(2,1)}, u32[]{:S(2)}, u32[]{:S(2)}) async-start(bf16[4,512,896]{2,1,0:T(8,128)(2,1)} %bitcast.83), calls=%async_computation.7 | async-start | bytes 7340032 | tf_op jit(solution)/shard_map/all_to_all | solution.py:53
  490.5 465.4 %all-reduce.2.cloned.1.call-start = ((), (), s32[]{:S(2)}) async-start(), calls=%async_computation.9 | async-start | bytes 524288 | tf_op jit(solution)/shard_map/psum | solution.py:18
  580.2 3.1 copy-start.3
  583.3 4.4 copy-start.2
  628.9 6.0 copy-start.5
  641.0 14.8 %copy-start = (bf16[512,3584]{1,0:T(8,128)(2,1)S(1)}, bf16[512,3584]{1,0:T(8,128)(2,1)}, u32[]{:S(2)}) copy-start(bf16[512,3584]{1,0:T(8,128)(2,1)} %get-tuple-element.712) | copy-start | bytes 11010052 | tf_op jit(solution)/shard_map/while
  669.3 4.8 collective-permute-start
  680.1 14.8 %copy-start = (bf16[512,3584]{1,0:T(8,128)(2,1)S(1)}, bf16[512,3584]{1,0:T(8,128)(2,1)}, u32[]{:S(2)}) copy-start(bf16[512,3584]{1,0:T(8,128)(2,1)} %get-tuple-element.712) | copy-start | bytes 11010052 | tf_op jit(solution)/shard_map/while
  708.5 6.2 collective-permute-start
  720.7 14.8 %copy-start = (bf16[512,3584]{1,0:T(8,128)(2,1)S(1)}, bf16[512,3584]{1,0:T(8,128)(2,1)}, u32[]{:S(2)}) copy-start(bf16[512,3584]{1,0:T(8,128)(2,1)} %get-tuple-element.712) | copy-start | bytes 11010052 | tf_op jit(solution)/shard_map/while
  749.0 6.2 collective-permute-start
  761.3 14.8 %copy-start = (bf16[512,3584]{1,0:T(8,128)(2,1)S(1)}, bf16[512,3584]{1,0:T(8,128)(2,1)}, u32[]{:S(2)}) copy-start(bf16[512,3584]{1,0:T(8,128)(2,1)} %get-tuple-element.712) | copy-start | bytes 11010052 | tf_op jit(solution)/shard_map/while
  789.6 6.2 collective-permute-start
  801.9 14.8 %copy-start = (bf16[512,3584]{1,0:T(8,128)(2,1)S(1)}, bf16[512,3584]{1,0:T(8,128)(2,1)}, u32[]{:S(2)}) copy-start(bf16[512,3584]{1,0:T(8,128)(2,1)} %get-tuple-element.712) | copy-start | bytes 11010052 | tf_op jit(solution)/shard_map/while
  830.2 6.2 collective-permute-start
  842.5 14.8 %copy-start = (bf16[512,3584]{1,0:T(8,128)(2,1)S(1)}, bf16[512,3584]{1,0:T(8,128)(2,1)}, u32[]{:S(2)}) copy-start(bf16[512,3584]{1,0:T(8,128)(2,1)} %get-tuple-element.712) | copy-start | bytes 11010052 | tf_op jit(solution)/shard_map/while
  870.8 6.2 collective-permute-start
  883.1 14.8 %copy-start = (bf16[512,3584]{1,0:T(8,128)(2,1)S(1)}, bf16[512,3584]{1,0:T(8,128)(2,1)}, u32[]{:S(2)}) copy-start(bf16[512,3584]{1,0:T(8,128)(2,1)} %get-tuple-element.712) | copy-start | bytes 11010052 | tf_op jit(solution)/shard_map/while
  911.4 6.2 collective-permute-start
Sparse Core Ops, SparseCore 0:
  918.5 37.3 all-reduce.1
